TPU v7x, 256 devices: a whole 4x4x8 slice. The times are simulated.
256 devices in a mesh: ctx: 64 (over z, x_hi, y), tp: 4 (over x_lo, core).
Axes of the slice: x: 4 (x_hi: 2, x_lo: 2; x = x_hi * 2 + x_lo), y: 4, z: 8, core: 2. Of those that a mesh axis runs over, the one named last changes fastest.
Arguments:
- query_raw: bfloat16 [32768, 2048], P('ctx', 'tp'), may hold values from -6 to 6
- key_unnormed: bfloat16 [32768, 1024], P('ctx', 'tp'), may hold values from -6 to 6
- value_matrix: bfloat16 [32768, 1024], P('ctx', 'tp'), may hold values from -6 to 6
- output_grad: bfloat16 [32768, 3840], P(('ctx', 'tp')), may hold values from -24 to 24
- output_weight: bfloat16 [3840, 2048], P('ctx', 'tp'), may hold values from -0.125 to 0.125
Outputs:
- query_grad: bfloat16 [32768, 2048], P('ctx', 'tp')
- key_raw_gradient: bfloat16 [32768, 1024], P('ctx', 'tp')
- value_rows_gradient: bfloat16 [32768, 1024], P('ctx', 'tp')
- weight_grad: float32 [3840, 2048], P('ctx', 'tp')
All inputs are finite; a program needn't handle non-finite values.
Results may differ from a plain program's by a relative error of at most 0.01.
Values may be sent and summed in bfloat16 or wider, within the bound.
No kernel may reach another device: no remote copies, remote signals or barrier semaphores. Data moves between devices by JAX's collectives and lax.ppermute only.
A program may use at most 128 MiB of HBM per device.

v0:
```python
import jax
import jax.numpy as jnp
from jax import lax
from jax.sharding import PartitionSpec as P

HEAD_SIZE = 256
WINDOW_TOKENS = 1024
EPSILON = 1e-06


def from_behind(block, axis, distance):
    devices = range(lax.axis_size(axis))
    route = [(i - distance, i) for i in devices if i - distance in devices]
    return lax.ppermute(block, axis, route)


def normalized_rows(raw, heads):
    token_total = raw.shape[0]
    widened = raw.astype(jnp.float32).reshape(token_total, heads, -1)
    factor = lax.rsqrt(jnp.mean(widened * widened, axis=-1, keepdims=True) + EPSILON)
    return (widened * factor, factor)


def normalized_backward(grad, normed, factor):
    return factor * (grad - normed * jnp.mean(grad * normed, axis=-1, keepdims=True))


def contract_last(left, right):
    return lax.dot_general(
        left, right, (((1,), (1,)), ((), ())), preferred_element_type=jnp.float32
    )


def contract_first(left, right):
    return lax.dot_general(
        left, right, (((0,), (0,)), ((), ())), preferred_element_type=jnp.float32
    )


def band_mask(query_count, key_total):
    query_index = lax.broadcasted_iota(jnp.int32, (query_count, key_total), 0)
    key_index = lax.broadcasted_iota(jnp.int32, (query_count, key_total), 1)
    return (key_index > query_index) & (key_index <= query_index + WINDOW_TOKENS)


def head_cols(array, index):
    return array[:, index * HEAD_SIZE : (index + 1) * HEAD_SIZE]


def body(query_raw, key_unnormed, value_matrix, output_grad, output_weight):
    block_rows = query_raw.shape[0]
    q_heads = query_raw.shape[1] // HEAD_SIZE
    kv_heads = key_unnormed.shape[1] // HEAD_SIZE
    query_group = q_heads // kv_heads
    reach_hops = WINDOW_TOKENS // block_rows
    scale = HEAD_SIZE ** (-0.5)
    q_unit, q_factor = normalized_rows(query_raw, q_heads)
    key_normalized, key_factor = normalized_rows(key_unnormed, kv_heads)
    q_norm = q_unit.astype(jnp.bfloat16).reshape(block_rows, -1)
    k_norm = key_normalized.astype(jnp.bfloat16).reshape(block_rows, -1)
    own_keys = jnp.concatenate([k_norm, value_matrix], axis=1)
    earlier = [from_behind(own_keys, "ctx", distance) for distance in range(reach_hops, 0, -1)]
    key_rows = jnp.concatenate(earlier + [own_keys], axis=0)
    key_total = key_rows.shape[0]
    split_at = kv_heads * HEAD_SIZE
    keys_all = key_rows[:, :split_at]
    values_all = key_rows[:, split_at:]
    first_key = lax.axis_index("ctx") * block_rows - WINDOW_TOKENS
    key_position = lax.broadcasted_iota(jnp.int32, (block_rows, key_total), 1) + first_key
    visible = band_mask(block_rows, key_total) & (key_position >= 0)
    grad_full = lax.all_gather(output_grad, "tp", axis=0, tiled=True)
    columns = grad_full
    grad_heads = jnp.dot(
        columns,
        lax.all_gather(output_weight, "ctx", axis=0, tiled=True),
        preferred_element_type=jnp.float32,
    ).astype(jnp.bfloat16)
    probs = []
    probs_low = []
    row_totals = []
    attended_list = []
    for head_index in range(q_heads):
        kv_index = head_index // query_group
        scores = contract_last(head_cols(q_norm, head_index), head_cols(keys_all, kv_index)) * scale
        weights_exp = jnp.where(visible, jnp.exp(scores), 0.0)
        row_total = jnp.sum(weights_exp, axis=1, keepdims=True)
        prob = weights_exp / row_total
        prob_reduced = prob.astype(jnp.bfloat16)
        attended_list.append(
            jnp.dot(
                prob_reduced, head_cols(values_all, kv_index), preferred_element_type=jnp.float32
            ).astype(jnp.bfloat16)
        )
        probs.append(prob)
        probs_low.append(prob_reduced)
        row_totals.append(row_total)
    attended = jnp.concatenate(attended_list, axis=1)
    columns = grad_full
    weight_grad = lax.psum_scatter(
        contract_first(columns, attended), "ctx", scatter_dimension=0, tiled=True
    )
    key_parts = [jnp.zeros((key_total, HEAD_SIZE), jnp.float32)]
    value_parts = [jnp.zeros((key_total, HEAD_SIZE), jnp.float32)]
    deltas = []
    query_grads = []
    for head_index in range(q_heads):
        kv_index = head_index // query_group
        grad_h = head_cols(grad_heads, head_index)
        delta = jnp.sum(
            grad_h.astype(jnp.float32) * attended_list[head_index].astype(jnp.float32),
            axis=1,
            keepdims=True,
        )
        grad_prob = contract_last(grad_h, head_cols(values_all, kv_index))
        score_gradient = (probs[head_index] * (grad_prob - delta) * scale).astype(jnp.bfloat16)
        query_grads.append(
            jnp.dot(
                score_gradient, head_cols(keys_all, kv_index), preferred_element_type=jnp.float32
            )
        )
        key_parts[kv_index] = key_parts[kv_index] + contract_first(
            score_gradient, head_cols(q_norm, head_index)
        )
        value_parts[kv_index] = value_parts[kv_index] + contract_first(
            probs_low[head_index], grad_h
        )
        deltas.append(delta)
    key_grads = jnp.concatenate(key_parts + value_parts, axis=1)
    combined = key_grads[WINDOW_TOKENS:]
    for distance in range(1, reach_hops + 1):
        lower = (reach_hops - distance) * block_rows
        combined = combined + from_behind(
            key_grads[lower : lower + block_rows].astype(jnp.bfloat16), "ctx", -distance
        ).astype(jnp.float32)
    q_grad_unit = jnp.concatenate(query_grads, axis=1).reshape(block_rows, q_heads, HEAD_SIZE)
    query_grad = (
        normalized_backward(q_grad_unit, q_unit, q_factor)
        .astype(jnp.bfloat16)
        .reshape(block_rows, -1)
    )
    k_grad_unit = combined[:, :split_at].reshape(block_rows, kv_heads, HEAD_SIZE)
    key_raw_gradient = (
        normalized_backward(k_grad_unit, key_normalized, key_factor)
        .astype(jnp.bfloat16)
        .reshape(block_rows, -1)
    )
    value_rows_gradient = combined[:, split_at:].astype(jnp.bfloat16)
    return (query_grad, key_raw_gradient, value_rows_gradient, weight_grad)


def solution(mesh):
    placed = (
        P("ctx", "tp"),
        P("ctx", "tp"),
        P("ctx", "tp"),
        P(("ctx", "tp"), None),
        P("ctx", "tp"),
    )
    return jax.shard_map(
        body,
        mesh=mesh,
        in_specs=placed,
        out_specs=(P("ctx", "tp"), P("ctx", "tp"), P("ctx", "tp"), P("ctx", "tp")),
        check_vma=False,
    )
```

profile of v0, /device:TPU:2, one launch (start us, length us, event | category | flops | bytes accessed | tf_op | source)
XLA Modules:
  0.0 958.2 jit_solution(6041601433919446470)
XLA Ops:
  7.2 0.7 all-gather.6.cloned.1.call-update
  8.0 0.7 all-gather.4.cloned.1.call-update
  8.7 1.1 copy.24
  9.8 1.1 copy.25
  11.1 3.5 collective-permute-start.1
  14.6 5.6 collective-permute-start
  20.2 0.2 copy.23
  20.7 6.2 collective-permute-done.1
  26.9 10.6 %collective-permute-done = bf16[512,512]{0,1:T(8,128)(2,1)} collective-permute-done((bf16[512,512]{0,1:T(8,128)(2,1)S(1)}, bf16[512,512]{0,1:T(8,128)(2,1)}, u32[]{:S(2)}, u32[]{:S(2)}) %collective-permute-start) | collective-permute-done | bytes 524320 | tf_op jit(solution)/shard_map/ppermute | solution.py:14
  37.5 1.1 maximum_maximum_fusion
  38.6 1.3 fusion.57
  40.0 2.9 fusion.56
  42.9 0.7 convolution_convert_fusion.1
  43.6 114.3 %all-gather.6.cloned.1.call-done = bf16[64,60,512]{2,1,0:T(8,128)(2,1)} async-done(((bf16[1,60,512]{2,1,0:T(8,128)(2,1)}), bf16[64,60,512]{2,1,0:T(8,128)(2,1)}) %all-gather.6.cloned.1.call-update) | async-done | bytes 3932176 | tf_op jit(solution)/shard_map/all_gather | solution.py:75
  157.9 6.3 reshape.75
  164.2 38.0 %all-gather.4.cloned.1.call-done = bf16[512,3840]{1,0:T(8,128)(2,1)} async-done(((bf16[128,3840]{1,0:T(8,128)(2,1)}), bf16[512,3840]{1,0:T(8,128)(2,1)}) %all-gather.4.cloned.1.call-update) | async-done | bytes 3932176 | tf_op jit(solution)/shard_map/all_gather | solution.py:71
  202.3 5.7 convolution_convert_fusion
  208.0 0.8 multiply_reduce_fusion.3
  208.8 1.5 copy-done.1
  210.3 5.4 convolution_bitcast_fusion
  215.7 0.6 copy-done.7
  216.3 0.6 dynamic-slice
  217.6 2.7 fusion.12
  220.3 0.6 fusion.47
  220.9 1.3 copy-done.9
  222.2 0.7 fusion.11
  222.9 0.6 convolution_add_fusion.1
  223.5 1.3 copy-done.11
  224.8 0.7 fusion.21
  225.5 0.7 convolution_add_fusion
  226.2 0.3 fusion.8
  226.5 1.1 fusion.55
  227.5 0.1 copy-done
  227.7 1.3 collective-permute-start.2
  229.0 1.3 collective-permute-start.3
  230.3 0.6 fusion.39
  230.9 0.6 fusion.42
  231.5 0.2 multiply_reduce_fusion
  231.7 0.2 fusion.13
  231.9 1.0 copy.26
  233.0 29.3 %collective-permute-done.2 = bf16[512,512]{0,1:T(8,128)(2,1)S(1)} collective-permute-done((bf16[512,512]{0,1:T(8,128)(2,1)}, bf16[512,512]{0,1:T(8,128)(2,1)S(1)}, u32[]{:S(2)}, u32[]{:S(2)}) %collective-permute-start.2) | collective-permute-done | bytes 524320 | tf_op jit(solution)/shard_map/ppermute | solution.py:14
  262.3 0.8 copy-done.5
  263.0 1.6 fusion.16
  264.7 0.8 copy.28
  265.7 0.8 copy.27
  266.6 683.1 %all-reduce.3.cloned.1.call-done = f32[3840,512]{0,1:T(8,128)} async-done(((f32[3840,512]{0,1:T(8,128)}), f32[3840,512]{0,1:T(8,128)}) %all-reduce.3.cloned.1.call-update) | async-done | bytes 7864336
  949.7 1.2 constant_dynamic-slice_fusion
  950.9 0.8 copy.29
  (41 shorter events, 0.9 us)
Async XLA Ops:
  7.2 13.1 %copy-start.6 = (bf16[512,512]{1,0:T(8,128)(2,1)S(1)}, bf16[512,512]{1,0:T(8,128)(2,1)}, u32[]{:S(2)}) copy-start(bf16[512,512]{1,0:T(8,128)(2,1)} %param.5) | copy-start | bytes 1572868
  7.2 150.7 %all-gather.6.cloned.1.call-start = ((), (), s32[]{:S(2)}) async-start(), calls=%async_computation.1 | async-start | bytes 4259840 | tf_op jit(solution)/shard_map/all_gather | solution.py:75
  7.9 194.4 %all-gather.4.cloned.1.call-start = ((), (), s32[]{:S(2)}) async-start(), calls=%async_computation | async-start | bytes 4915200 | tf_op jit(solution)/shard_map/all_gather | solution.py:71
  8.7 941.1 %all-reduce.3.cloned.1.call-start = ((), (), s32[]{:S(2)}) async-start(), calls=%async_computation.2 | async-start | bytes 15728640
  11.1 15.8 %collective-permute-start.1 = (bf16[512,512]{0,1:T(8,128)(2,1)S(1)}, bf16[512,512]{0,1:T(8,128)(2,1)S(1)}, u32[]{:S(2)}, u32[]{:S(2)}) collective-permute-start(bf16[512,512]{0,1:T(8,128)(2,1)S(1)} %pad_maximum_fusion.2), channel_id=1, source_target_pairs={{0,4},{4,8},{8,12},{12,16},{16,20},{20,24},{24,28},{28,32},{32,36}... | collective-permute-start | bytes 1572872 | tf_op jit(solution)/shard_map/ppermute | solution.py:14
  14.6 22.9 %collective-permute-start = (bf16[512,512]{0,1:T(8,128)(2,1)S(1)}, bf16[512,512]{0,1:T(8,128)(2,1)}, u32[]{:S(2)}, u32[]{:S(2)}) collective-permute-start(bf16[512,512]{0,1:T(8,128)(2,1)S(1)} %pad_maximum_fusion.2), channel_id=1, source_target_pairs={{0,8},{4,12},{8,16},{12,20},{16,24},{20,28},{24,32},{28,36},{32,40... | collective-permute-start | bytes 1572872 | tf_op jit(solution)/shard_map/ppermute | solution.py:14
  38.6 4.2 copy-start.2
  40.0 2.9 copy-start.8
  164.2 43.7 %copy-start.3 = (bf16[1536,512]{0,1:T(8,128)(2,1)S(1)}, bf16[1536,512]{0,1:T(8,128)(2,1)}, u32[]{:S(2)}) copy-start(bf16[1536,512]{0,1:T(8,128)(2,1)} %copy-done.2) | copy-start | bytes 4718596
  202.3 5.7 copy-start.10
  208.0 0.8 copy-start.12
  208.0 2.3 copy-start.1
  215.6 0.7 copy-start.7
  217.6 3.3 copy-start.13
  220.3 1.9 copy-start.9
  222.9 1.9 copy-start.11
  226.2 1.5 copy-start
  226.2 4.1 copy-start.4
  227.7 34.6 %collective-permute-start.2 = (bf16[512,512]{0,1:T(8,128)(2,1)}, bf16[512,512]{0,1:T(8,128)(2,1)S(1)}, u32[]{:S(2)}, u32[]{:S(2)}) collective-permute-start(bf16[512,512]{0,1:T(8,128)(2,1)} %get-tuple-element.18), channel_id=1, source_target_pairs={{4,0},{8,4},{12,8},{16,12},{20,16},{24,20},{28,24},{32,28},{36,32}... | collective-permute-start | bytes 1572872 | tf_op jit(solution)/shard_map/ppermute | solution.py:14
  229.0 34.1 %collective-permute-start.3 = (bf16[512,512]{0,1:T(8,128)(2,1)}, bf16[512,512]{0,1:T(8,128)(2,1)}, u32[]{:S(2)}, u32[]{:S(2)}) collective-permute-start(bf16[512,512]{0,1:T(8,128)(2,1)} %get-tuple-element.19), channel_id=1, source_target_pairs={{8,0},{12,4},{16,8},{20,12},{24,16},{28,20},{32,24},{36,28},{40,32... | collective-permute-start | bytes 1572872 | tf_op jit(solution)/shard_map/ppermute | solution.py:14
  262.3 0.8 copy-start.5
Sparse Core Ops, SparseCore 0:
  11.5 146.3 all-gather.5
  159.7 42.5 all-gather.3
  215.8 733.8 all-reduce.2
where the time goes:
time: 959 us; the launch traced here: 958 us
  waiting for transfers between devices  883 us (92%)
  matrix products  23.9 us (2%)
  local copies, waits for them, and re-layouts  20.7 us (2%)
  between operations  14.7 us (2%)
  starting transfers between devices  11.8 us (1%)
    unnamed x4, waiting for transfers between devices  685 us
    all_gather x1, waiting for transfers between devices, body(): lax.all_gather(output_weight, 'ctx', axis=0, tiled=True)  114 us
    ppermute x4, waiting for transfers between devices, from_behind(): return lax.ppermute(block, axis, route)  46.1 us
    all_gather x1, waiting for transfers between devices, body(): grad_full = lax.all_gather(output_grad, 'tp', axis=0, tiled=True)  38 us
    unnamed x38, local copies, waits for them, and re-layouts  19.6 us
  transfers between devices with their start and end apart: 7, of which 6 were waited for; matrix products, arithmetic and copies ran while one was open for 3% of the time, Pallas kernels for 0%

commit v1 on v0

--- a/solution.py
+++ b/solution.py
@@ -72,7 +72,9 @@
     columns = grad_full
     grad_heads = jnp.dot(
         columns,
-        lax.all_gather(output_weight, "ctx", axis=0, tiled=True),
+        jnp.concatenate(
+            lax.all_to_all(jnp.stack([output_weight] * lax.axis_size("ctx")), "ctx", 0, 0), axis=0
+        ),
         preferred_element_type=jnp.float32,
     ).astype(jnp.bfloat16)
     probs = []

time: 959 us -> 915 us (0.954)
  waiting for transfers between devices: 883 us -> 824 us
  starting transfers between devices: 11.8 us -> 25.5 us
    all_gather x1 -> x0, waiting for transfers between devices: 114 us -> none  [body(): lax.all_gather(output_weight, 'ctx', axis=0, tiled=True)]
    unnamed x4 -> x3, waiting for transfers between devices: 685 us -> 726 us
    all_to_all x0 -> x1, waiting for transfers between devices: none -> 39.9 us  [body(): lax.all_to_all(jnp.stack([output_weight] * lax.axis_size('ctx')), 'ctx',...]
    all_gather x1, waiting for transfers between devices: 38 us -> 0.01 us  [body(): grad_full = lax.all_gather(output_grad, 'tp', axis=0, tiled=True)]
    all_to_all x0 -> x1, starting transfers between devices: none -> 14.1 us  [body(): lax.all_to_all(jnp.stack([output_weight] * lax.axis_size('ctx')), 'ctx',...]
    ppermute x4, waiting for transfers between devices: 46.1 us -> 58.4 us  [from_behind(): return lax.ppermute(block, axis, route)]
    unnamed x38 -> x39, local copies, waits for them, and re-layouts: 19.6 us -> 10.7 us
where the time goes in v1:
time: 915 us; the launch traced here: 914 us
  waiting for transfers between devices  824 us (90%)
  starting transfers between devices  25.5 us (3%)
  matrix products  23.9 us (3%)
  local copies, waits for them, and re-layouts  21.4 us (2%)
  between operations  15.1 us (2%)
    unnamed x3, waiting for transfers between devices  726 us
    ppermute x4, waiting for transfers between devices, from_behind(): return lax.ppermute(block, axis, route)  58.4 us
    all_to_all x1, waiting for transfers between devices, body(): lax.all_to_all(jnp.stack([output_weight] * lax.axis_size('ctx')), 'ctx',...  39.9 us
  transfers between devices with their start and end apart: 7, of which 6 were waited for; matrix products, arithmetic and copies ran while one was open for 3% of the time, Pallas kernels for 0%

profile of v1, /device:TPU:2, one launch (start us, length us, event | category | flops | bytes accessed | tf_op | source)
XLA Modules:
  0.0 914.0 jit_solution(5841510415229113156)
XLA Ops:
  7.2 3.3 stack.2
  10.5 14.1 %all-to-all-start = ((bf16[64,60,512]{2,1,0:T(8,128)(2,1)}), bf16[64,60,512]{2,1,0:T(8,128)(2,1)}, u32[]{:S(2)}, u32[]{:S(2)}) async-start(bf16[64,60,512]{2,1,0:T(8,128)(2,1)} %stack.2), calls=%async_computation | async-start | bytes 8388608 | tf_op jit(solution)/shard_map/all_to_all | solution.py:76
  24.6 0.7 all-gather.2.cloned.1.call-update
  25.4 0.1 copy.25
  25.5 0.1 copy.24
  25.9 3.4 collective-permute-start.1
  29.3 5.4 collective-permute-start
  34.7 0.2 copy.23
  35.2 19.6 %collective-permute-done.1 = bf16[512,512]{0,1:T(8,128)(2,1)S(1)} collective-permute-done((bf16[512,512]{0,1:T(8,128)(2,1)S(1)}, bf16[512,512]{0,1:T(8,128)(2,1)S(1)}, u32[]{:S(2)}, u32[]{:S(2)}) %collective-permute-start.1) | collective-permute-done | bytes 524320 | tf_op jit(solution)/shard_map/ppermute | solution.py:14
  54.7 19.1 %collective-permute-done = bf16[512,512]{0,1:T(8,128)(2,1)} collective-permute-done((bf16[512,512]{0,1:T(8,128)(2,1)S(1)}, bf16[512,512]{0,1:T(8,128)(2,1)}, u32[]{:S(2)}, u32[]{:S(2)}) %collective-permute-start) | collective-permute-done | bytes 524320 | tf_op jit(solution)/shard_map/ppermute | solution.py:14
  73.8 1.1 maximum_maximum_fusion
  74.9 1.3 fusion.57
  76.3 2.9 fusion.56
  79.1 0.7 convolution_convert_fusion.1
  79.9 39.9 %all-to-all-done = bf16[64,60,512]{2,1,0:T(8,128)(2,1)} async-done(((bf16[64,60,512]{2,1,0:T(8,128)(2,1)}), bf16[64,60,512]{2,1,0:T(8,128)(2,1)}, u32[]{:S(2)}, u32[]{:S(2)}) %all-to-all-start) | async-done | bytes 3932192 | tf_op jit(solution)/shard_map/all_to_all | solution.py:76
  119.8 6.3 reshape.78
  126.1 5.7 convolution_convert_fusion
  131.9 0.8 multiply_reduce_fusion.3
  132.6 1.5 copy-done.1
  134.1 5.4 convolution_bitcast_fusion
  139.5 0.6 copy-done.8
  140.2 0.6 dynamic-slice
  141.4 2.7 fusion.12
  144.2 0.6 fusion.47
  144.7 1.3 copy-done.10
  146.0 0.7 fusion.11
  146.8 0.6 convolution_add_fusion.1
  147.4 1.3 copy-done.12
  148.7 0.7 fusion.21
  149.4 0.7 convolution_add_fusion
  150.1 0.3 fusion.8
  150.4 1.0 fusion.55
  151.4 0.2 copy-done
  151.6 1.3 collective-permute-start.3
  152.8 1.3 collective-permute-start.2
  154.2 0.6 fusion.39
  154.8 0.6 fusion.42
  155.4 0.2 multiply_reduce_fusion
  155.6 0.2 fusion.13
  155.8 1.0 copy.26
  156.8 9.7 %collective-permute-done.3 = bf16[512,512]{0,1:T(8,128)(2,1)S(1)} collective-permute-done((bf16[512,512]{0,1:T(8,128)(2,1)}, bf16[512,512]{0,1:T(8,128)(2,1)S(1)}, u32[]{:S(2)}, u32[]{:S(2)}) %collective-permute-start.3) | collective-permute-done | bytes 524320 | tf_op jit(solution)/shard_map/ppermute | solution.py:14
  166.5 10.2 %collective-permute-done.2 = bf16[512,512]{0,1:T(8,128)(2,1)} collective-permute-done((bf16[512,512]{0,1:T(8,128)(2,1)}, bf16[512,512]{0,1:T(8,128)(2,1)}, u32[]{:S(2)}, u32[]{:S(2)}) %collective-permute-start.2) | collective-permute-done | bytes 524320 | tf_op jit(solution)/shard_map/ppermute | solution.py:14
  176.7 1.4 fusion.16
  178.4 0.8 copy.27
  179.2 0.8 copy.28
  180.0 725.1 %all-reduce.3.cloned.1.call-done = f32[3840,512]{0,1:T(8,128)} async-done(((f32[3840,512]{0,1:T(8,128)}), f32[3840,512]{0,1:T(8,128)}) %all-reduce.3.cloned.1.call-update) | async-done | bytes 7864336
  905.2 1.2 constant_dynamic-slice_fusion
  906.3 0.8 copy.29
  (43 shorter events, 0.8 us)
Async XLA Ops:
  10.5 14.9 %copy-start.6 = (bf16[512,256]{1,0:T(8,128)(2,1)S(1)}, bf16[512,256]{1,0:T(8,128)(2,1)}, u32[]{:S(2)}) copy-start(bf16[512,256]{1,0:T(8,128)(2,1)} %param.7) | copy-start | bytes 786436
  10.5 15.0 %copy-start.7 = (bf16[512,256]{1,0:T(8,128)(2,1)S(1)}, bf16[512,256]{1,0:T(8,128)(2,1)}, u32[]{:S(2)}) copy-start(bf16[512,256]{1,0:T(8,128)(2,1)} %param.6) | copy-start | bytes 786436
  10.5 109.3 %all-to-all-start = ((bf16[64,60,512]{2,1,0:T(8,128)(2,1)}), bf16[64,60,512]{2,1,0:T(8,128)(2,1)}, u32[]{:S(2)}, u32[]{:S(2)}) async-start(bf16[64,60,512]{2,1,0:T(8,128)(2,1)} %stack.2), calls=%async_computation | async-start | bytes 8388608 | tf_op jit(solution)/shard_map/all_to_all | solution.py:76
  24.5 10.1 %copy-start.5 = (bf16[512,512]{1,0:T(8,128)(2,1)S(1)}, bf16[512,512]{1,0:T(8,128)(2,1)}, u32[]{:S(2)}) copy-start(bf16[512,512]{1,0:T(8,128)(2,1)} %param.5) | copy-start | bytes 1572868
  24.6 101.6 %all-gather.2.cloned.1.call-start = ((), (), s32[]{:S(2)}) async-start(), calls=%async_computation.1 | async-start | bytes 4915200 | tf_op jit(solution)/shard_map/all_gather | solution.py:71
  25.3 879.9 %all-reduce.3.cloned.1.call-start = ((), (), s32[]{:S(2)}) async-start(), calls=%async_computation.2 | async-start | bytes 15728640
  25.9 28.9 %collective-permute-start.1 = (bf16[512,512]{0,1:T(8,128)(2,1)S(1)}, bf16[512,512]{0,1:T(8,128)(2,1)S(1)}, u32[]{:S(2)}, u32[]{:S(2)}) collective-permute-start(bf16[512,512]{0,1:T(8,128)(2,1)S(1)} %pad_maximum_fusion.2), channel_id=1, source_target_pairs={{0,4},{4,8},{8,12},{12,16},{16,20},{20,24},{24,28},{28,32},{32,36}... | collective-permute-start | bytes 1572872 | tf_op jit(solution)/shard_map/ppermute | solution.py:14
  29.3 44.5 %collective-permute-start = (bf16[512,512]{0,1:T(8,128)(2,1)S(1)}, bf16[512,512]{0,1:T(8,128)(2,1)}, u32[]{:S(2)}, u32[]{:S(2)}) collective-permute-start(bf16[512,512]{0,1:T(8,128)(2,1)S(1)} %pad_maximum_fusion.2), channel_id=1, source_target_pairs={{0,8},{4,12},{8,16},{12,20},{16,24},{20,28},{24,32},{28,36},{32,40... | collective-permute-start | bytes 1572872 | tf_op jit(solution)/shard_map/ppermute | solution.py:14
  74.9 4.2 copy-start.2
  76.3 2.9 copy-start.9
  126.1 5.7 copy-start.3
  126.1 5.7 copy-start.11
  131.8 0.8 copy-start.13
  131.9 2.3 copy-start.1
  139.5 0.7 copy-start.8
  141.4 3.3 copy-start.14
  144.1 1.9 copy-start.10
  146.8 1.9 copy-start.12
  150.1 1.5 copy-start
  150.1 4.1 copy-start.4
  151.6 14.9 %collective-permute-start.3 = (bf16[512,512]{0,1:T(8,128)(2,1)}, bf16[512,512]{0,1:T(8,128)(2,1)S(1)}, u32[]{:S(2)}, u32[]{:S(2)}) collective-permute-start(bf16[512,512]{0,1:T(8,128)(2,1)} %get-tuple-element.19), channel_id=1, source_target_pairs={{8,0},{12,4},{16,8},{20,12},{24,16},{28,20},{32,24},{36,28},{40,32... | collective-permute-start | bytes 1572872 | tf_op jit(solution)/shard_map/ppermute | solution.py:14
  152.8 23.8 %collective-permute-start.2 = (bf16[512,512]{0,1:T(8,128)(2,1)}, bf16[512,512]{0,1:T(8,128)(2,1)}, u32[]{:S(2)}, u32[]{:S(2)}) collective-permute-start(bf16[512,512]{0,1:T(8,128)(2,1)} %get-tuple-element.18), channel_id=1, source_target_pairs={{4,0},{8,4},{12,8},{16,12},{20,16},{24,20},{28,24},{32,28},{36,32}... | collective-permute-start | bytes 1572872 | tf_op jit(solution)/shard_map/ppermute | solution.py:14
Sparse Core Ops, SparseCore 0:
  27.2 75.9 all-gather.1
  139.7 765.4 all-reduce.2
